TPU v7x, 512 devices: a whole 4x8x8 slice. The times are simulated.
512 devices in a mesh: dp: 4 (over x), expert: 128 (over z, y, core).
Axes of the slice: x: 4, y: 8, z: 8, core: 2. Of those that a mesh axis runs over, the one named last changes fastest.
Arguments:
- tokens: bfloat16 [8192, 2048], P(('dp', 'expert')), may hold values from -6 to 6
- cotangent: bfloat16 [8192, 2048], P(('dp', 'expert')), may hold values from -6 to 6
- routes: int32 [8192, 8], P(('dp', 'expert')), may hold values from 0 to 127, all different within a row; in each aligned block of 16 rows (0 to 15, 16 to 31, ...) at most 2 rows name the same one
- gate_values: float32 [8192, 8], P(('dp', 'expert')), may hold values from 0.1 to 1
- gate_weight: bfloat16 [128, 768, 2048], P('expert', 'dp'), may hold values from -0.125 to 0.125
- up_weight: bfloat16 [128, 768, 2048], P('expert', 'dp'), may hold values from -0.125 to 0.125
- down_weight: bfloat16 [128, 768, 2048], P('expert', None, 'dp'), may hold values from -0.21875 to 0.21875
Outputs:
- mixed: bfloat16 [8192, 2048], P(('dp', 'expert'))
- grad_gate_weight: bfloat16 [128, 768, 2048], P('expert', 'dp')
- grad_up_weight: bfloat16 [128, 768, 2048], P('expert', 'dp')
- grad_down_weight: bfloat16 [128, 768, 2048], P('expert', None, 'dp')
Inputs may be any that keep to these rules, and one draw needn't show every extreme that they name: `routes`: each row names 8 different experts. Among the rows of one device no expert is named more than 2 times, and in some device's rows some expert is named exactly 2 times.
All inputs are finite; a program needn't handle non-finite values.
Results may differ from a plain program's by a relative error of at most 0.0058.
Values may be sent and summed in bfloat16 or wider, within the bound.
A program may use at most 64 MiB of HBM per device.

v0:
```python
import jax
import jax.numpy as jnp
from jax import lax
from jax.sharding import PartitionSpec as P


def body(tokens, cotangent, routes, gate_values, gate_weight, up_weight, down_weight):
    tok_rows = tokens.shape[0]
    width = tokens.shape[1]
    top_count = routes.shape[1]
    experts = lax.axis_size("expert")
    groups = lax.axis_size("dp")
    capacity = min(tok_rows, max(2, 2 * tok_rows * top_count // experts))
    onehot = routes[:, :, None] == jnp.arange(experts, dtype=jnp.int32)[None, None, :]
    named = jnp.sum(onehot.astype(jnp.int32), axis=1)
    earlier = jnp.cumsum(named, axis=0) - named
    slot_ids = jnp.arange(capacity, dtype=jnp.int32)[None, :, None]
    placer = (named.T[:, None, :] == 1) & (earlier.T[:, None, :] == slot_ids)
    placer_half = placer.astype(jnp.bfloat16)
    placer_full = placer.astype(jnp.float32)
    token_gate = jnp.sum(
        jnp.where(onehot, gate_values[:, :, None], jnp.zeros((), jnp.float32)), axis=1
    )
    slot_gate = jnp.sum(placer_full * token_gate.T[:, None, :], axis=2)
    row_input = jnp.einsum(
        "est,td->esd", placer_half, tokens, preferred_element_type=jnp.float32
    ).astype(jnp.bfloat16)
    picked_cot = jnp.einsum(
        "est,td->esd", placer_half, cotangent, preferred_element_type=jnp.float32
    )
    row_cot = (slot_gate[:, :, None] * picked_cot).astype(jnp.bfloat16)
    arrived_input, arrived_cot = (
        lax.all_to_all(row_input, "expert", split_axis=0, concat_axis=0, tiled=True),
        lax.all_to_all(row_cot, "expert", split_axis=0, concat_axis=0, tiled=True),
    )
    local_rows = arrived_input.shape[0] * arrived_input.shape[1]
    flat_input = arrived_input.reshape(local_rows, width)
    flat_cot = arrived_cot.reshape(local_rows, width)
    gate_local = gate_weight[0]
    up_local = up_weight[0]
    down_local = down_weight[0]
    quarter_width = down_local.shape[1]
    inputs_all = lax.all_gather(flat_input, "dp", axis=0, tiled=True)
    cot_quarter = lax.all_to_all(flat_cot, "dp", split_axis=1, concat_axis=0, tiled=True)
    contract_last = (((1,), (1,)), ((), ()))
    gate_pre = lax.dot_general(
        gate_local, inputs_all, contract_last, preferred_element_type=jnp.float32
    )
    up_pre = lax.dot_general(
        up_local, inputs_all, contract_last, preferred_element_type=jnp.float32
    )
    hidden_part = (jax.nn.silu(gate_pre) * up_pre).astype(jnp.bfloat16)
    hidden_all = lax.all_gather(hidden_part, "dp", axis=0, tiled=True)
    contract_lead = (((0,), (0,)), ((), ()))
    expert_out = lax.dot_general(
        hidden_all, down_local, contract_lead, preferred_element_type=jnp.float32
    ).astype(jnp.bfloat16)
    grad_down = jnp.dot(hidden_all, cot_quarter, preferred_element_type=jnp.float32).astype(
        jnp.bfloat16
    )
    grad_hidden = lax.psum_scatter(
        lax.dot_general(down_local, cot_quarter, contract_last, preferred_element_type=jnp.float32),
        "dp",
        scatter_dimension=0,
        tiled=True,
    )
    sigma = jax.nn.sigmoid(gate_pre)
    grad_gate = (grad_hidden * up_pre * sigma * (1.0 + gate_pre * (1.0 - sigma))).astype(
        jnp.bfloat16
    )
    grad_up = (grad_hidden * jax.nn.silu(gate_pre)).astype(jnp.bfloat16)
    grad_gate_local = jnp.dot(grad_gate, inputs_all, preferred_element_type=jnp.float32).astype(
        jnp.bfloat16
    )
    grad_up_local = jnp.dot(grad_up, inputs_all, preferred_element_type=jnp.float32).astype(
        jnp.bfloat16
    )
    out_blocks = expert_out.reshape(groups, experts, capacity, quarter_width)
    returned = lax.all_to_all(
        lax.all_to_all(out_blocks, "dp", split_axis=0, concat_axis=3, tiled=True),
        "expert",
        split_axis=1,
        concat_axis=1,
        tiled=True,
    )
    returned_rows = returned.reshape(experts * capacity, width).astype(jnp.float32)
    combine_rows = (placer_full * slot_gate[:, :, None]).reshape(experts * capacity, tok_rows)
    mixed = lax.dot_general(
        combine_rows,
        returned_rows,
        contract_lead,
        precision=lax.Precision.HIGHEST,
        preferred_element_type=jnp.float32,
    ).astype(jnp.bfloat16)
    return (mixed, grad_gate_local[None], grad_up_local[None], grad_down[None])


def solution(mesh):
    in_specs = (
        P(("dp", "expert"), None),
        P(("dp", "expert"), None),
        P(("dp", "expert"), None),
        P(("dp", "expert"), None),
        P("expert", "dp", None),
        P("expert", "dp", None),
        P("expert", None, "dp"),
    )
    out_specs = (
        P(("dp", "expert"), None),
        P("expert", "dp", None),
        P("expert", "dp", None),
        P("expert", None, "dp"),
    )
    return jax.shard_map(body, mesh=mesh, in_specs=in_specs, out_specs=out_specs, check_vma=False)
```

profile of v0, /device:TPU:1, one launch (start us, length us, event | category | flops | bytes accessed | tf_op | source)
XLA Modules:
  0.0 236.6 jit_solution(17935731720747272963)
XLA Ops:
  7.2 0.8 copy.53
  8.2 0.8 copy.56
  9.4 0.3 select_reduce_fusion
  9.8 1.3 convolution_convert_fusion
  11.1 1.1 copy.59
  12.2 49.3 %all_to_all.52 = bf16[128,2,2048]{2,1,0:T(2,128)(2,1)S(1)} all-to-all(bf16[128,2,2048]{2,1,0:T(2,128)(2,1)S(1)} %copy.59), channel_id=1, replica_groups=mesh['dp'=4,'expert'=128] {'expert'}, dimensions={0} | all-to-all | bytes 2097152 | tf_op jit(solution)/shard_map/all_to_all | solution.py:33
  61.4 1.2 reshape.91
  62.7 0.5 fusion
  63.2 2.1 copy.65
  65.3 6.5 %all-to-all-start.3 = ((bf16[128,2,2048]{2,1,0:T(2,128)(2,1)}), bf16[128,2,2048]{2,1,0:T(2,128)(2,1)S(1)}, u32[]{:S(2)}, u32[]{:S(2)}) async-start(bf16[128,2,2048]{2,1,0:T(2,128)(2,1)} %copy.65), calls=%async_computation.3 | async-start | bytes 2097152 | tf_op jit(solution)/shard_map/all_to_all | solution.py:34
  71.8 38.1 %all-gather.3.cloned.1.call-done = bf16[1024,2048]{1,0:T(8,128)(2,1)} async-done(((bf16[256,2048]{1,0:T(8,128)(2,1)}), bf16[1024,2048]{1,0:T(8,128)(2,1)}) %all-gather.3.cloned.1.call-update) | async-done | bytes 4194320 | tf_op jit(solution)/shard_map/all_gather | solution.py:43
  110.0 3.9 %convolution_bitcast_fusion.2 = f32[192,1024]{1,0:T(8,128)S(1)} fusion(bf16[1024,2048]{1,0:T(8,128)(2,1)} %all-gather.3.cloned.1.call-done, bf16[1,192,2048]{2,1,0:T(8,128)(2,1)S(1)} %copy-done.5), kind=kOutput, calls=%fused_computation.13 | convolution fusion | flops 805306368 | bytes 5767168 | tf_op jit(solution)/shard_map/dot_general | solution.py:46
  113.9 2.6 %multiply_convert_fusion.2 = (bf16[192,1024]{1,0:T(8,128)(2,1)}, f32[192,1024]{1,0:T(8,128)}) fusion(f32[192,1024]{1,0:T(8,128)S(1)} %convolution_bitcast_fusion.2, bf16[1024,2048]{1,0:T(8,128)(2,1)S(1)} %copy-done.2, bf16[1,192,2048]{2,1,0:T(8,128)(2,1)S(1)} %copy-done.6), kind=kOutput, calls=%fused_computation.20 | convolution fusion | flops 806486016 | bytes 6946816 | tf_op jit(solution)/shard_map/dot_general | solution.py:49
  116.6 0.7 all_to_all.43
  117.3 0.2 copy.66
  117.5 17.0 %all_to_all.53 = bf16[256,4,512]{2,0,1:T(8,128)(2,1)S(1)} all-to-all(bf16[256,4,512]{2,0,1:T(8,128)(2,1)S(1)} %copy.66), channel_id=1, replica_groups=mesh['dp'=4,'expert'=128] {'dp'}, dimensions={1} | all-to-all | bytes 2097152 | tf_op jit(solution)/shard_map/all_to_all | solution.py:44
  134.5 2.7 %convolution_bitcast_fusion = f32[768,1024]{1,0:T(8,128)} fusion(bf16[1024,512]{1,0:T(8,128)(2,1)S(1)} %bitcast.59, bf16[1,768,512]{2,1,0:T(8,128)(2,1)S(1)} %copy-done), kind=kOutput, calls=%fused_computation.8 | convolution fusion | flops 805306368 | bytes 4980736 | tf_op jit(solution)/shard_map/dot_general | solution.py:62
  137.3 11.7 %all-gather.5.cloned.1.call-done = bf16[768,1024]{1,0:T(8,128)(2,1)} async-done(((bf16[192,1024]{1,0:T(8,128)(2,1)}), bf16[768,1024]{1,0:T(8,128)(2,1)}) %all-gather.5.cloned.1.call-update) | async-done | bytes 1572880 | tf_op jit(solution)/shard_map/all_gather | solution.py:53
  148.9 3.4 %convolution_convert_fusion.4 = bf16[1024,512]{1,0:T(8,128)(2,1)} fusion(bf16[768,1024]{1,0:T(8,128)(2,1)} %all-gather.5.cloned.1.call-done, bf16[1,768,512]{2,1,0:T(8,128)(2,1)S(1)} %copy-done), kind=kOutput, calls=%fused_computation.9 | convolution fusion | flops 805830656 | bytes 3407872 | tf_op jit(solution)/shard_map/dot_general | solution.py:55
  152.3 1.5 reshape.92
  153.8 2.0 copy.60
  155.8 21.9 %all_to_all.54 = bf16[4,128,2,512]{1,3,2,0:T(8,128)(2,1)S(1)} all-to-all(bf16[4,128,2,512]{1,3,2,0:T(8,128)(2,1)} %copy.60), channel_id=1, replica_groups=mesh['dp'=4,'expert'=128] {'dp'}, dimensions={0} | all-to-all | bytes 2097152 | tf_op jit(solution)/shard_map/all_to_all | solution.py:80
  177.7 2.1 copy.62
  179.8 17.7 %all-to-all-start.2 = ((bf16[1,128,2,2048]{3,2,0,1:T(2,128)(2,1)}), bf16[1,128,2,2048]{3,2,0,1:T(2,128)(2,1)S(1)}, u32[]{:S(2)}, u32[]{:S(2)}) async-start(bf16[1,128,2,2048]{3,2,0,1:T(2,128)(2,1)} %copy.62), calls=%async_computation.2 | async-start | bytes 2097152 | tf_op jit(solution)/shard_map/all_to_all | solution.py:79
  197.5 0.2 broadcast_select_fusion
  197.7 3.4 %reduce-scatter.2.cloned.1.call-done = f32[192,1024]{1,0:T(8,128)} async-done(((f32[768,1024]{1,0:T(8,128)}), f32[192,1024]{1,0:T(8,128)}) %reduce-scatter.2.cloned.1.call-update) | async-done | bytes 786448 | tf_op jit(solution)/shard_map/reduce_scatter | solution.py:61
  201.2 4.7 %fusion.2 = bf16[1,192,2048]{2,1,0:T(8,128)(2,1)} fusion(bf16[1024,2048]{1,0:T(8,128)(2,1)} %all-gather.3.cloned.1.call-done, f32[192,1024]{1,0:T(8,128)} %reduce-scatter.2.cloned.1.call-done, f32[192,1024]{1,0:T(8,128)} %copy-done.8), kind=kOutput, calls=%fused_computation.6 | convolution fusion | flops 806879232 | bytes 6553600 | tf_op jit(solution)/shard_map/dot_general | solution.py:75
  205.9 2.0 fusion.1
  208.0 1.9 fusion.3
  209.8 18.6 %all-to-all-done.2 = bf16[1,128,2,2048]{3,2,0,1:T(2,128)(2,1)S(1)} async-done(((bf16[1,128,2,2048]{3,2,0,1:T(2,128)(2,1)}), bf16[1,128,2,2048]{3,2,0,1:T(2,128)(2,1)S(1)}, u32[]{:S(2)}, u32[]{:S(2)}) %all-to-all-start.2) | async-done | bytes 1048608 | tf_op jit(solution)/shard_map/all_to_all | solution.py:79
  228.4 0.4 reshape.93
  228.9 1.2 convolution_convert_fusion.3
  (40 shorter events, 1.0 us)
Async XLA Ops:
  7.2 127.4 %copy-start = (bf16[1,768,512]{2,1,0:T(8,128)(2,1)S(1)}, bf16[1,768,512]{2,1,0:T(8,128)(2,1)}, u32[]{:S(2)}) copy-start(bf16[1,768,512]{2,1,0:T(8,128)(2,1)} %param.13) | copy-start | bytes 2359300
  7.2 102.8 %all-gather.3.cloned.1.call-start = ((), (), s32[]{:S(2)}) async-start(), calls=%async_computation.6 | async-start | bytes 5242880 | tf_op jit(solution)/shard_map/all_gather | solution.py:43
  12.2 50.6 %copy-start.1 = (bf16[16,2048]{1,0:T(8,128)(2,1)S(1)}, bf16[16,2048]{1,0:T(8,128)(2,1)}, u32[]{:S(2)}) copy-start(bf16[16,2048]{1,0:T(8,128)(2,1)} %param.8) | copy-start | bytes 196612
  62.6 47.3 %copy-start.5 = (bf16[1,192,2048]{2,1,0:T(8,128)(2,1)S(1)}, bf16[1,192,2048]{2,1,0:T(8,128)(2,1)}, u32[]{:S(2)}) copy-start(bf16[1,192,2048]{2,1,0:T(8,128)(2,1)} %param.11) | copy-start | bytes 2359300
  65.3 51.3 %all-to-all-start.3 = ((bf16[128,2,2048]{2,1,0:T(2,128)(2,1)}), bf16[128,2,2048]{2,1,0:T(2,128)(2,1)S(1)}, u32[]{:S(2)}, u32[]{:S(2)}) async-start(bf16[128,2,2048]{2,1,0:T(2,128)(2,1)} %copy.65), calls=%async_computation.3 | async-start | bytes 2097152 | tf_op jit(solution)/shard_map/all_to_all | solution.py:34
  71.8 42.0 %copy-start.6 = (bf16[1,192,2048]{2,1,0:T(8,128)(2,1)S(1)}, bf16[1,192,2048]{2,1,0:T(8,128)(2,1)}, u32[]{:S(2)}) copy-start(bf16[1,192,2048]{2,1,0:T(8,128)(2,1)} %param.12) | copy-start | bytes 2359300
  71.8 77.1 %all-gather.5.cloned.1.call-start = ((), (), s32[]{:S(2)}) async-start(), calls=%async_computation.7 | async-start | bytes 1966080 | tf_op jit(solution)/shard_map/all_gather | solution.py:53
  110.0 3.9 %copy-start.2 = (bf16[1024,2048]{1,0:T(8,128)(2,1)S(1)}, bf16[1024,2048]{1,0:T(8,128)(2,1)}, u32[]{:S(2)}) copy-start(bf16[1024,2048]{1,0:T(8,128)(2,1)} %all-gather.3.cloned.1.call-done) | copy-start | bytes 12582916
  113.8 2.6 %copy-start.8 = (f32[192,1024]{1,0:T(8,128)}, f32[192,1024]{1,0:T(8,128)S(1)}, u32[]{:S(2)}) copy-start(f32[192,1024]{1,0:T(8,128)S(1)} %convolution_bitcast_fusion.2) | copy-start | bytes 2359300
  116.5 84.6 %reduce-scatter.2.cloned.1.call-start = ((), (), s32[]{:S(2)}) async-start(), calls=%async_computation.8 | async-start | bytes 3932160 | tf_op jit(solution)/shard_map/reduce_scatter | solution.py:61
  179.8 48.6 %all-to-all-start.2 = ((bf16[1,128,2,2048]{3,2,0,1:T(2,128)(2,1)}), bf16[1,128,2,2048]{3,2,0,1:T(2,128)(2,1)S(1)}, u32[]{:S(2)}, u32[]{:S(2)}) async-start(bf16[1,128,2,2048]{3,2,0,1:T(2,128)(2,1)} %copy.62), calls=%async_computation.2 | async-start | bytes 2097152 | tf_op jit(solution)/shard_map/all_to_all | solution.py:79
  201.2 4.7 %copy-start.3 = (bf16[1024,2048]{1,0:T(8,128)(2,1)S(1)}, bf16[1024,2048]{1,0:T(8,128)(2,1)}, u32[]{:S(2)}) copy-start(bf16[1024,2048]{1,0:T(8,128)(2,1)} %all-gather.3.cloned.1.call-done) | copy-start | bytes 12582916
  201.2 4.7 %copy-start.7 = (f32[192,1024]{1,0:T(8,128)S(1)}, f32[192,1024]{1,0:T(8,128)}, u32[]{:S(2)}) copy-start(f32[192,1024]{1,0:T(8,128)} %reduce-scatter.2.cloned.1.call-done) | copy-start | bytes 2359300
  201.2 4.7 %copy-start.9 = (f32[192,1024]{1,0:T(8,128)S(1)}, f32[192,1024]{1,0:T(8,128)}, u32[]{:S(2)}) copy-start(f32[192,1024]{1,0:T(8,128)} %copy-done.8) | copy-start | bytes 2359300
  201.2 4.7 %copy-start.10 = (f32[192,1024]{1,0:T(8,128)S(1)}, f32[192,1024]{1,0:T(8,128)}, u32[]{:S(2)}) copy-start(f32[192,1024]{1,0:T(8,128)} %get-tuple-element.7) | copy-start | bytes 2359300
  205.9 2.1 copy-start.4
Sparse Core Ops, SparseCore 0:
  62.8 47.1 all-gather.2
  116.6 32.2 all-gather.4
  151.8 49.3 reduce-scatter.1
where the time goes:
time: 237 us
  blocking collectives  88.2 us (37%)
  waiting for transfers between devices  71.9 us (30%)
  starting transfers between devices  24.3 us (10%)
  matrix products  24.2 us (10%)
  between operations  13.9 us (6%)
  local copies, waits for them, and re-layouts  13.4 us (6%)
    all_to_all x1, blocking collectives, body(): lax.all_to_all(row_input, 'expert', split_axis=0, concat_axis=0, tiled=True)  49.3 us
    all_gather x1, waiting for transfers between devices, body(): inputs_all = lax.all_gather(flat_input, 'dp', axis=0, tiled=True)  38.1 us
    all_to_all x1, blocking collectives, body(): lax.all_to_all(out_blocks, 'dp', split_axis=0, concat_axis=3, tiled=True)  21.9 us
    all_to_all x1, waiting for transfers between devices, body(): lax.all_to_all(lax.all_to_all(out_blocks, 'dp', split_axis=0, concat_axis...  18.6 us
    all_to_all x1, starting transfers between devices, body(): lax.all_to_all(lax.all_to_all(out_blocks, 'dp', split_axis=0, concat_axis...  17.7 us
    all_to_all x1, blocking collectives, body(): lax.all_to_all(flat_cot, 'dp', split_axis=1, concat_axis=0, tiled=True)  17 us
    all_gather x1, waiting for transfers between devices, body(): hidden_all = lax.all_gather(hidden_part, 'dp', axis=0, tiled=True)  11.7 us
    all_to_all x1, starting transfers between devices, body(): lax.all_to_all(row_cot, 'expert', split_axis=0, concat_axis=0, tiled=True)  6.48 us
  transfers between devices with their start and end apart: 5, of which 4 were waited for; matrix products, arithmetic and copies ran while one was open for 13% of the time, Pallas kernels for 0%

commit v1 on v0

--- a/solution.py
+++ b/solution.py
@@ -50,7 +50,10 @@
         up_local, inputs_all, contract_last, preferred_element_type=jnp.float32
     )
     hidden_part = (jax.nn.silu(gate_pre) * up_pre).astype(jnp.bfloat16)
-    hidden_all = lax.all_gather(hidden_part, "dp", axis=0, tiled=True)
+    size = lax.axis_size("dp")
+    parts = jnp.stack([hidden_part for _ in range(size)])
+    parts = lax.all_to_all(parts, "dp", split_axis=0, concat_axis=0)
+    hidden_all = jnp.concatenate(parts, axis=0)
     contract_lead = (((0,), (0,)), ((), ()))
     expert_out = lax.dot_general(
         hidden_all, down_local, contract_lead, preferred_element_type=jnp.float32

time: 237 us -> 247 us (1.042)
  blocking collectives: 88.2 us -> 152 us
  waiting for transfers between devices: 71.9 us -> 22.1 us
  starting transfers between devices: 24.3 us -> 19.7 us
    all_to_all x0 -> x2, blocking collectives: none -> 70 us  [the longest x1 37.2 us: body(): lax.all_to_all(row_cot, 'expert', split_axis=0, concat_axis=0, tiled=True)]
    all_gather x1, waiting for transfers between devices: 38.1 us -> 0.02 us  [body(): inputs_all = lax.all_gather(flat_input, 'dp', axis=0, tiled=True)]
    all_gather x1 -> x0, waiting for transfers between devices: 11.7 us -> none  [body(): hidden_all = lax.all_gather(hidden_part, 'dp', axis=0, tiled=True)]
    all_to_all x1, blocking collectives: 21.9 us -> 14.9 us  [body(): lax.all_to_all(out_blocks, 'dp', split_axis=0, concat_axis=3, tiled=True)]
    all_to_all x1 -> x0, starting transfers between devices: 6.48 us -> none  [body(): lax.all_to_all(row_cot, 'expert', split_axis=0, concat_axis=0, tiled=True)]
    reduce_scatter x1, waiting for transfers between devices: 3.43 us -> 0.02 us  [body(): lax.psum_scatter(lax.dot_general(down_local, cot_quarter, contract_last,...]
    all_to_all x1, waiting for transfers between devices: 18.6 us -> 22 us  [body(): lax.all_to_all(lax.all_to_all(out_blocks, 'dp', split_axis=0, concat_axis...]
  transfers between devices with their start and end apart: 5 -> 3, of which waited for: 4 -> 1; matrix products, arithmetic and copies ran while one was open for 13% -> 11% of each run, Pallas kernels for 0% -> 0%
where the time goes in v1:
time: 247 us
  blocking collectives  152 us (62%)
  matrix products  22.7 us (9%)
  waiting for transfers between devices  22.1 us (9%)
  starting transfers between devices  19.7 us (8%)
  local copies, waits for them, and re-layouts  15 us (6%)
  between operations  14.3 us (6%)
    all_to_all x1, blocking collectives, body(): lax.all_to_all(row_input, 'expert', split_axis=0, concat_axis=0, tiled=True)  49.1 us
    all_to_all x1, blocking collectives, body(): lax.all_to_all(row_cot, 'expert', split_axis=0, concat_axis=0, tiled=True)  37.2 us
    all_to_all x1, blocking collectives, body(): parts = lax.all_to_all(parts, 'dp', split_axis=0, concat_axis=0)  32.8 us
    all_to_all x1, waiting for transfers between devices, body(): lax.all_to_all(lax.all_to_all(out_blocks, 'dp', split_axis=0, concat_axis...  22 us
    all_to_all x1, starting transfers between devices, body(): lax.all_to_all(lax.all_to_all(out_blocks, 'dp', split_axis=0, concat_axis...  19.6 us
    all_to_all x1, blocking collectives, body(): lax.all_to_all(flat_cot, 'dp', split_axis=1, concat_axis=0, tiled=True)  18.4 us
    all_to_all x1, blocking collectives, body(): lax.all_to_all(out_blocks, 'dp', split_axis=0, concat_axis=3, tiled=True)  14.9 us
  transfers between devices with their start and end apart: 3, of which 1 were waited for; matrix products, arithmetic and copies ran while one was open for 11% of the time, Pallas kernels for 0%

profile of v1, /device:TPU:1, one launch (start us, length us, event | category | flops | bytes accessed | tf_op | source)
XLA Modules:
  0.0 246.8 jit_solution(8992099329016142953)
XLA Ops:
  7.2 0.8 copy.53
  8.2 0.8 copy.56
  9.4 0.3 select_reduce_fusion
  9.8 1.3 convolution_convert_fusion
  11.1 1.1 copy.59
  12.2 49.1 %all_to_all.57 = bf16[128,2,2048]{2,1,0:T(2,128)(2,1)S(1)} all-to-all(bf16[128,2,2048]{2,1,0:T(2,128)(2,1)S(1)} %copy.59), channel_id=1, replica_groups=mesh['dp'=4,'expert'=128] {'expert'}, dimensions={0} | all-to-all | bytes 2097152 | tf_op jit(solution)/shard_map/all_to_all | solution.py:33
  61.3 1.2 reshape.96
  62.7 0.5 fusion
  63.2 1.1 copy.65
  64.3 37.2 %all_to_all.58 = bf16[128,2,2048]{2,1,0:T(2,128)(2,1)S(1)} all-to-all(bf16[128,2,2048]{2,1,0:T(2,128)(2,1)S(1)} %copy.65), channel_id=1, replica_groups=mesh['dp'=4,'expert'=128] {'expert'}, dimensions={0} | all-to-all | bytes 2097152 | tf_op jit(solution)/shard_map/all_to_all | solution.py:34
  101.4 0.7 all_to_all.47
  102.1 0.2 copy.66
  102.3 18.4 %all_to_all.59 = bf16[256,4,512]{2,0,1:T(8,128)(2,1)S(1)} all-to-all(bf16[256,4,512]{2,0,1:T(8,128)(2,1)S(1)} %copy.66), channel_id=1, replica_groups=mesh['dp'=4,'expert'=128] {'dp'}, dimensions={1} | all-to-all | bytes 2097152 | tf_op jit(solution)/shard_map/all_to_all | solution.py:44
  120.8 2.7 %convolution_bitcast_fusion = f32[768,1024]{1,0:T(8,128)} fusion(bf16[1024,512]{1,0:T(8,128)(2,1)S(1)} %bitcast.60, bf16[1,768,512]{2,1,0:T(8,128)(2,1)S(1)} %copy-done), kind=kOutput, calls=%fused_computation.8 | convolution fusion | flops 805306368 | bytes 4980736 | tf_op jit(solution)/shard_map/dot_general | solution.py:65
  123.5 1.1 copy-done.6
  124.6 3.9 %convolution_bitcast_fusion.2 = f32[192,1024]{1,0:T(8,128)S(1)} fusion(bf16[1024,2048]{1,0:T(8,128)(2,1)} %all-gather.2.cloned.1.call-done, bf16[1,192,2048]{2,1,0:T(8,128)(2,1)S(1)} %copy-done.6), kind=kOutput, calls=%fused_computation.13 | convolution fusion | flops 805306368 | bytes 5767168 | tf_op jit(solution)/shard_map/dot_general | solution.py:46
  128.5 2.5 %multiply_convert_fusion.2 = (bf16[192,1024]{1,0:T(8,128)(2,1)S(1)}, f32[192,1024]{1,0:T(8,128)}) fusion(f32[192,1024]{1,0:T(8,128)S(1)} %convolution_bitcast_fusion.2, bf16[1024,2048]{1,0:T(8,128)(2,1)S(1)} %copy-done.4, bf16[1,192,2048]{2,1,0:T(8,128)(2,1)S(1)} %copy-done.7), kind=kOutput, calls=%fused_computation.20 | convolution fusion | flops 806486016 | bytes 6946816 | tf_op jit(solution)/shard_map/dot_general | solution.py:49
  131.2 32.8 %all_to_all.60 = bf16[4,192,1024]{2,1,0:T(8,128)(2,1)S(1)} all-to-all(bf16[4,192,1024]{2,1,0:T(8,128)(2,1)S(1)} %stack.2), channel_id=1, replica_groups=mesh['dp'=4,'expert'=128] {'dp'}, dimensions={0} | all-to-all | bytes 3145728 | tf_op jit(solution)/shard_map/all_to_all | solution.py:55
  164.0 1.2 copy-done.1
  165.3 2.0 convolution_convert_fusion.4
  167.3 1.5 reshape.98
  168.7 2.0 copy.60
  170.8 14.9 %all_to_all.61 = bf16[4,128,2,512]{1,3,2,0:T(8,128)(2,1)S(1)} all-to-all(bf16[4,128,2,512]{1,3,2,0:T(8,128)(2,1)} %copy.60), channel_id=1, replica_groups=mesh['dp'=4,'expert'=128] {'dp'}, dimensions={0} | all-to-all | bytes 2097152 | tf_op jit(solution)/shard_map/all_to_all | solution.py:83
  185.8 2.1 copy.62
  187.8 19.6 %all-to-all-start.3 = ((bf16[1,128,2,2048]{3,2,0,1:T(2,128)(2,1)}), bf16[1,128,2,2048]{3,2,0,1:T(2,128)(2,1)S(1)}, u32[]{:S(2)}, u32[]{:S(2)}) async-start(bf16[1,128,2,2048]{3,2,0,1:T(2,128)(2,1)} %copy.62), calls=%async_computation.3 | async-start | bytes 2097152 | tf_op jit(solution)/shard_map/all_to_all | solution.py:82
  207.5 0.2 broadcast_select_fusion
  207.7 4.7 %fusion.2 = bf16[1,192,2048]{2,1,0:T(8,128)(2,1)} fusion(bf16[1024,2048]{1,0:T(8,128)(2,1)} %all-gather.2.cloned.1.call-done, f32[192,1024]{1,0:T(8,128)} %reduce-scatter.2.cloned.1.call-done, f32[192,1024]{1,0:T(8,128)} %copy-done.9), kind=kOutput, calls=%fused_computation.6 | convolution fusion | flops 806879232 | bytes 6553600 | tf_op jit(solution)/shard_map/dot_general | solution.py:78
  212.5 2.0 fusion.1
  214.5 1.9 fusion.3
  216.4 22.0 %all-to-all-done.3 = bf16[1,128,2,2048]{3,2,0,1:T(2,128)(2,1)S(1)} async-done(((bf16[1,128,2,2048]{3,2,0,1:T(2,128)(2,1)}), bf16[1,128,2,2048]{3,2,0,1:T(2,128)(2,1)S(1)}, u32[]{:S(2)}, u32[]{:S(2)}) %all-to-all-start.3) | async-done | bytes 1048608 | tf_op jit(solution)/shard_map/all_to_all | solution.py:82
  238.4 0.4 reshape.99
  238.8 1.2 convolution_convert_fusion.3
  (40 shorter events, 1.2 us)
Async XLA Ops:
  7.2 113.6 %copy-start = (bf16[1,768,512]{2,1,0:T(8,128)(2,1)S(1)}, bf16[1,768,512]{2,1,0:T(8,128)(2,1)}, u32[]{:S(2)}) copy-start(bf16[1,768,512]{2,1,0:T(8,128)(2,1)} %param.13) | copy-start | bytes 2359300
  7.2 116.4 %all-gather.2.cloned.1.call-start = ((), (), s32[]{:S(2)}) async-start(), calls=%async_computation.7 | async-start | bytes 5242880 | tf_op jit(solution)/shard_map/all_gather | solution.py:43
  61.3 1.4 copy-start.3
  62.6 145.1 %reduce-scatter.2.cloned.1.call-start = ((), (), s32[]{:S(2)}) async-start(), calls=%async_computation.8 | async-start | bytes 3932160 | tf_op jit(solution)/shard_map/reduce_scatter | solution.py:64
  123.5 1.1 copy-start.6
  123.5 5.0 %copy-start.7 = (bf16[1,192,2048]{2,1,0:T(8,128)(2,1)S(1)}, bf16[1,192,2048]{2,1,0:T(8,128)(2,1)}, u32[]{:S(2)}) copy-start(bf16[1,192,2048]{2,1,0:T(8,128)(2,1)} %param.12) | copy-start | bytes 2359300
  124.6 3.9 %copy-start.4 = (bf16[1024,2048]{1,0:T(8,128)(2,1)S(1)}, bf16[1024,2048]{1,0:T(8,128)(2,1)}, u32[]{:S(2)}) copy-start(bf16[1024,2048]{1,0:T(8,128)(2,1)} %all-gather.2.cloned.1.call-done) | copy-start | bytes 12582916
  128.5 2.5 %copy-start.9 = (f32[192,1024]{1,0:T(8,128)}, f32[192,1024]{1,0:T(8,128)S(1)}, u32[]{:S(2)}) copy-start(f32[192,1024]{1,0:T(8,128)S(1)} %convolution_bitcast_fusion.2) | copy-start | bytes 2359300
  164.0 1.2 copy-start.1
  187.8 50.5 %all-to-all-start.3 = ((bf16[1,128,2,2048]{3,2,0,1:T(2,128)(2,1)}), bf16[1,128,2,2048]{3,2,0,1:T(2,128)(2,1)S(1)}, u32[]{:S(2)}, u32[]{:S(2)}) async-start(bf16[1,128,2,2048]{3,2,0,1:T(2,128)(2,1)} %copy.62), calls=%async_computation.3 | async-start | bytes 2097152 | tf_op jit(solution)/shard_map/all_to_all | solution.py:82
  207.7 4.8 %copy-start.5 = (bf16[1024,2048]{1,0:T(8,128)(2,1)S(1)}, bf16[1024,2048]{1,0:T(8,128)(2,1)}, u32[]{:S(2)}) copy-start(bf16[1024,2048]{1,0:T(8,128)(2,1)} %all-gather.2.cloned.1.call-done) | copy-start | bytes 12582916
  207.7 4.8 %copy-start.8 = (f32[192,1024]{1,0:T(8,128)S(1)}, f32[192,1024]{1,0:T(8,128)}, u32[]{:S(2)}) copy-start(f32[192,1024]{1,0:T(8,128)} %reduce-scatter.2.cloned.1.call-done) | copy-start | bytes 2359300
  207.7 4.7 %copy-start.10 = (f32[192,1024]{1,0:T(8,128)S(1)}, f32[192,1024]{1,0:T(8,128)}, u32[]{:S(2)}) copy-start(f32[192,1024]{1,0:T(8,128)} %copy-done.9) | copy-start | bytes 2359300
  207.7 4.7 %copy-start.11 = (f32[192,1024]{1,0:T(8,128)S(1)}, f32[192,1024]{1,0:T(8,128)}, u32[]{:S(2)}) copy-start(f32[192,1024]{1,0:T(8,128)} %get-tuple-element.7) | copy-start | bytes 2359300
  212.5 2.0 copy-start.2
Sparse Core Ops, SparseCore 0:
  62.7 47.1 all-gather.1
  123.6 58.5 reduce-scatter.1
